TPU v7x, 256 devices: a whole 4x4x8 slice. The times are simulated.
256 devices in a mesh: seq: 4 (over x), row: 2 (over core), col: 32 (over z, y).
Axes of the slice: x: 4, y: 4, z: 8, core: 2. Of those that a mesh axis runs over, the one named last changes fastest.
Arguments:
- activations: bfloat16 [2048, 16384], P('seq', ('row', 'col')), may hold values from -1500 to 1500
- norm_gain: float32 [16384], P(('row', 'col')), may hold values from 0.1 to 1.9
- query_weight: bfloat16 [16384, 8192], P('row', 'col'), may hold values from -0.046875 to 0.046875
- kv_weight: bfloat16 [16384, 2, 512], P('row'), may hold values from -0.046875 to 0.046875
- out_weight: bfloat16 [8192, 16384], P('col', 'row'), may hold values from -0.5 to 0.5
- block_ids: int32 [2048], replicated, may hold values from 0 to 255, never falling along the last dimension, each value on 1 to 16 neighbouring positions
- clean_mask: int32 [2048], replicated, may hold values 0 or 1
Outputs:
- layer_out: bfloat16 [2048, 16384], P('seq', ('row', 'col'))
Inputs may be any that keep to these rules, and one draw needn't show every extreme that they name: `block_ids`: block numbers never fall along the sequence; every block holds 1 to 16 tokens and one holds exactly 16.
All inputs are finite; a program needn't handle non-finite values.
Results may differ from a plain program's by a relative error of at most 0.009.
Values may be sent and summed in bfloat16 or wider, within the bound.
A program may use at most 128 MiB of HBM per device.

v0:
```python
import math

import jax
import jax.numpy as jnp
from jax import lax
from jax.sharding import PartitionSpec as P

D = 16384
HD = 128
QH = 64
KVH = 4


rope_base = 500000.0
norm_eps = 1e-05


def rotate(values, positions):
    half_dim = values.shape[-1] // 2
    inverse = jnp.exp(
        jnp.arange(half_dim, dtype=jnp.float32) * (-2.0 * math.log(rope_base) / values.shape[-1])
    )
    angles = positions.astype(jnp.float32)[:, None] * inverse[None, :]
    cosine = jnp.cos(angles)
    sine_part = jnp.sin(angles)
    first_half = values[..., :half_dim]
    second_half = values[..., half_dim:]
    return jnp.concatenate(
        [
            first_half * cosine - second_half * sine_part,
            second_half * cosine + first_half * sine_part,
        ],
        axis=-1,
    )


def shards(activations, norm_gain, query_weight, kv_weight, out_weight, block_ids, clean_mask):
    row_count = lax.axis_size("row")
    col_index = lax.axis_index("col")
    seq_index = lax.axis_index("seq")
    slab_len = activations.shape[0]
    col_heads = query_weight.shape[1] // HD
    dev_heads = col_heads // row_count
    group_size = QH // KVH
    wide_input = activations.astype(jnp.float32)
    squares = lax.psum(jnp.sum(wide_input * wide_input, axis=1), ("row", "col"))
    scaling = lax.rsqrt(squares / D + norm_eps)
    normed = (wide_input * scaling[:, None] * norm_gain[None, :]).astype(jnp.bfloat16)
    panel_rows = lax.all_gather(normed, "col", axis=1, tiled=True)
    kv_count = max(col_heads // group_size, 1)
    kv_first = col_index * col_heads // group_size
    kv_tiles = lax.dynamic_slice_in_dim(kv_weight, kv_first * HD, kv_count * HD, 2)
    kv_term = jnp.einsum("td,dke->kte", panel_rows, kv_tiles, preferred_element_type=jnp.float32)
    columns = query_weight
    columns = columns.reshape(columns.shape[0], dev_heads * lax.axis_size("row"), HD)
    query_sum = lax.psum_scatter(
        jnp.einsum("td,dhe->hte", panel_rows, columns, preferred_element_type=jnp.float32),
        "row",
        scatter_dimension=0,
        tiled=True,
    )
    kv_sum = lax.psum(kv_term, "row")
    key_raw = kv_sum[0]
    value_rows = kv_sum[1].astype(jnp.bfloat16)
    positions = seq_index * slab_len + jnp.arange(slab_len, dtype=jnp.int32)
    key_rows = rotate(key_raw, positions).astype(jnp.bfloat16)
    queries = rotate(query_sum, positions).astype(jnp.bfloat16)
    my_blocks = lax.dynamic_slice_in_dim(block_ids, seq_index * slab_len, slab_len, 0)
    score_scale = 1.0 / math.sqrt(HD)
    key_piece = lax.all_gather(key_rows, "seq", axis=0, tiled=True)
    value_piece = lax.all_gather(value_rows, "seq", axis=0, tiled=True)
    visible = (block_ids[None, :] == my_blocks[:, None]) | (
        block_ids[None, :] < my_blocks[:, None]
    ) & (clean_mask[None, :] == 1)
    scores = (
        jnp.einsum("hte,ne->htn", queries, key_piece, preferred_element_type=jnp.float32)
        * score_scale
    )
    weights = jnp.where(visible[None, :, :], jnp.exp(scores), jnp.zeros_like(scores))
    numerator = jnp.einsum(
        "htn,ne->hte", weights.astype(jnp.bfloat16), value_piece, preferred_element_type=jnp.float32
    )
    denominator = jnp.sum(weights, axis=2)
    numerator, denominator = (numerator, denominator)
    attended = (numerator / denominator[:, :, None]).astype(jnp.bfloat16)
    out_cols = out_weight.shape[1]
    portion = lax.all_gather(attended, "row", axis=0, tiled=True)
    heads_here = portion.shape[0]
    out_rows = out_weight
    out_rows = out_rows.reshape(heads_here, HD, out_cols)
    partial_out = jnp.einsum("hte,hed->td", portion, out_rows, preferred_element_type=jnp.float32)
    projected = lax.psum_scatter(partial_out, "col", scatter_dimension=1, tiled=True)
    return projected.astype(jnp.bfloat16)


def solution(mesh):
    placed = (
        P("seq", ("row", "col")),
        P(("row", "col")),
        P("row", "col"),
        P("row", None, None),
        P("col", "row"),
        P(),
        P(),
    )
    return jax.shard_map(
        shards, mesh=mesh, in_specs=placed, out_specs=P("seq", ("row", "col")), check_vma=False
    )
```

profile of v0, /device:TPU:1, one launch (start us, length us, event | category | flops | bytes accessed | tf_op | source)
XLA Modules:
  0.0 585.8 jit_solution(13208035812554895426)
XLA Ops:
  6.5 1.1 fusion.25
  7.6 133.5 %psum.14 = f32[512]{0:T(512)S(1)} all-reduce(f32[512]{0:T(512)S(1)} %fusion.25), channel_id=1, replica_groups=mesh['seq'=4,'row'=2,'col'=32] {'row','col'}, use_global_device_ids=true, to_apply=%region_1.0 | all-reduce | flops 512 | bytes 4096 | tf_op jit(solution)/shard_map/psum | solution.py:46
  141.1 1.8 fusion.27
  142.9 0.0 all-reduce.2.cloned.1.call-start
  143.0 0.8 dynamic_slice.6
  143.8 0.7 broadcast_compare_fusion
  144.5 7.8 %constant_dynamic-slice_fusion = bf16[8192,2,128]{2,1,0:T(2,128)(2,1)} fusion(bf16[8192,2,512]{2,1,0:T(2,128)(2,1)} %param.10, s32[]{:T(128)S(6)} %select_n.18), kind=kLoop, calls=%fused_computation.53 | loop fusion | bytes 8388612 | tf_op jit(solution)/shard_map/dynamic_slice | solution.py:52
  152.3 98.1 %all-gather.4.cloned.1.call-done = bf16[512,8192]{1,0:T(8,128)(2,1)} async-done(((bf16[512,256]{1,0:T(8,128)(2,1)}), bf16[512,8192]{1,0:T(8,128)(2,1)}) %all-gather.4.cloned.1.call-update) | async-done | bytes 8388624 | tf_op jit(solution)/shard_map/all_gather | solution.py:49
  250.4 7.9 %fusion.14 = f32[2,512,128]{1,2,0:T(8,128)} fusion(bf16[512,8192]{1,0:T(8,128)(2,1)} %all-gather.4.cloned.1.call-done, bf16[8192,2,128]{2,1,0:T(2,128)(2,1)} %constant_dynamic-slice_fusion), kind=kOutput, calls=%fused_computation.12 | convolution fusion | flops 2147483648 | bytes 13107200 | tf_op jit(solution)/shard_map/td,dke->kte/dot_general | solution.py:53
  258.3 0.0 reduce-scatter.3.cloned.1.call-start
  258.3 7.8 %fusion.9 = f32[2,512,128]{2,1,0:T(8,128)} fusion(bf16[512,8192]{1,0:T(8,128)(2,1)} %all-gather.4.cloned.1.call-done, bf16[8192,256]{1,0:T(8,128)(2,1)} %param.9), kind=kOutput, calls=%fused_computation.11 | convolution fusion | flops 2147483648 | bytes 13107200 | tf_op jit(solution)/shard_map/td,dhe->hte/dot_general | solution.py:57
  266.2 24.3 %all-reduce.2.cloned.1.call-done = f32[2,512,128]{1,2,0:T(8,128)} async-done(((f32[2,512,128]{1,2,0:T(8,128)}), f32[2,512,128]{1,2,0:T(8,128)}) %all-reduce.2.cloned.1.call-update) | async-done | bytes 524304 | tf_op jit(solution)/shard_map/psum | solution.py:62
  290.6 1.0 slice.49
  291.5 1.0 slice_bitcast_fusion
  292.5 0.6 fusion.42
  293.1 10.7 %all_gather.13 = bf16[2048,128]{0,1:T(8,128)(2,1)S(1)} all-gather(bf16[512,128]{0,1:T(8,128)(2,1)S(1)} %pad_maximum_fusion), channel_id=1, replica_groups=mesh['seq'=4,'row'=2,'col'=32] {'seq'}, dimensions={0}, use_global_device_ids=true | all-gather | bytes 655360 | tf_op jit(solution)/shard_map/all_gather | solution.py:70
  303.8 9.9 %all-gather = bf16[1,2048,128]{1,2,0:T(8,128)(2,1)S(1)} all-gather(bf16[1,512,128]{1,2,0:T(8,128)(2,1)S(1)} %slice.49), channel_id=2, replica_groups=mesh['seq'=4,'row'=2,'col'=32] {'seq'}, dimensions={1}, use_global_device_ids=true | all-gather | bytes 655360 | tf_op jit(solution)/shard_map/all_gather | solution.py:71
  313.7 2.2 fusion.49
  315.9 2.0 fusion.51
  317.9 0.7 fusion.22
  318.6 7.2 %all-gather.1 = bf16[1024,128]{1,0:T(8,128)(2,1)S(1)} all-gather(bf16[512,128]{1,0:T(8,128)(2,1)S(1)} %fusion.22), channel_id=3, replica_groups=mesh['seq'=4,'row'=2,'col'=32] {'row'}, dimensions={0}, use_global_device_ids=true | all-gather | bytes 393216 | tf_op jit(solution)/shard_map/all_gather | solution.py:87
  325.9 7.0 %convolution_bitcast_fusion = f32[512,8192]{1,0:T(8,128)} fusion(bf16[2,512,128]{2,1,0:T(8,128)(2,1)S(1)} %bitcast.40, bf16[2,128,8192]{2,1,0:T(8,128)(2,1)S(1)} %bitcast.39), kind=kOutput, calls=%fused_computation | convolution fusion | flops 2147483648 | bytes 21233664 | tf_op jit(solution)/shard_map/hte,hed->td/dot_general | solution.py:91
  332.8 244.6 %reduce-scatter.5.cloned.1.call-done = f32[512,256]{1,0:T(8,128)} async-done(((f32[512,8192]{1,0:T(8,128)}), f32[512,256]{1,0:T(8,128)}) %reduce-scatter.5.cloned.1.call-update) | async-done | bytes 524304 | tf_op jit(solution)/shard_map/reduce_scatter | solution.py:92
  577.5 1.8 convert_element_type.43
  (15 shorter events, 0.2 us)
Async XLA Ops:
  6.5 243.9 %all-gather.4.cloned.1.call-start = ((), (), s32[]{:S(2)}) async-start(), calls=%async_computation.2 | async-start | bytes 8650752 | tf_op jit(solution)/shard_map/all_gather | solution.py:49
  142.9 147.6 %all-reduce.2.cloned.1.call-start = ((), (), s32[]{:S(2)}) async-start(), calls=%async_computation.4 | async-start | bytes 1048576 | tf_op jit(solution)/shard_map/psum | solution.py:62
  258.3 57.6 %copy-start.1 = (s32[2048]{0:T(1024)S(1)}, s32[2048]{0:T(1024)}, u32[]{:S(2)}) copy-start(s32[2048]{0:T(1024)} %param.12) | copy-start | bytes 24580
  258.3 55.4 %reduce-scatter.3.cloned.1.call-start = ((), (), s32[]{:S(2)}) async-start(), calls=%async_computation.3 | async-start | bytes 786432 | tf_op jit(solution)/shard_map/reduce_scatter | solution.py:56
  266.1 311.3 %reduce-scatter.5.cloned.1.call-start = ((), (), s32[]{:S(2)}) async-start(), calls=%async_computation.5 | async-start | bytes 17301504 | tf_op jit(solution)/shard_map/reduce_scatter | solution.py:92
  315.9 10.0 %copy-start = (bf16[256,8192]{1,0:T(8,128)(2,1)S(1)}, bf16[256,8192]{1,0:T(8,128)(2,1)}, u32[]{:S(2)}) copy-start(bf16[256,8192]{1,0:T(8,128)(2,1)} %param.11) | copy-start | bytes 12582916
Sparse Core Ops, SparseCore 0:
  143.1 107.2 all-gather.3
  258.4 32.1 all-reduce.1
  293.1 14.5 reduce-scatter.2
  333.0 244.4 reduce-scatter.4
where the time goes:
time: 590 us; the launch traced here: 586 us
  waiting for transfers between devices  367 us (62%)
  blocking collectives  161 us (27%)
  matrix products  25.3 us (4%)
  between operations  13.2 us (2%)
  local copies, waits for them, and re-layouts  10.5 us (2%)
  other arithmetic  8.15 us (1%)
    reduce_scatter x1, waiting for transfers between devices, shards(): lax.psum_scatter(partial_out, 'col', scatter_dimension=1, tiled=True)  245 us
    psum x1, blocking collectives, shards(): squares = lax.psum(jnp.sum(wide_input * wide_input, axis=1), ('row', 'col'))  133 us
    all_gather x1, waiting for transfers between devices, shards(): panel_rows = lax.all_gather(normed, 'col', axis=1, tiled=True)  98.1 us
    psum x1, waiting for transfers between devices, shards(): kv_sum = lax.psum(kv_term, 'row')  24.3 us
  transfers between devices with their start and end apart: 4, of which 3 were waited for; matrix products, arithmetic and copies ran while one was open for 3% of the time, Pallas kernels for 0%

commit v1 on v0

v1 whole, which is shorter than its diff:
```python
import heapq
import math

import jax
import jax.numpy as jnp
import numpy as np
from jax import lax
from jax.experimental import pallas as pl
from jax.experimental.pallas import tpu as pltpu
from jax.sharding import PartitionSpec as P

D = 16384
HD = 128
QH = 64
KVH = 4
rope_base = 500000.0
norm_eps = 1e-05

MESH = pl.DeviceIdType.MESH
F32 = jnp.float32
BF16 = jnp.bfloat16

NZ, NY = 8, 4
SLAB = 512
SPLIT = 208
ROWS = ((0, SPLIT), (SPLIT, SLAB - SPLIT))
CH = 256


def norm(n):
    return (n[0] % NZ, n[1] % NY)


def slot(n):
    return (n[0] % NZ) * NY + n[1] % NY


def make_tree(part):
    parent = {}

    def ring(start, axis, size, sign):
        for direction, hops in ((sign, size // 2), (-sign, size // 2 - 1)):
            at = start
            for _ in range(hops):
                step = (direction, 0) if axis == 0 else (0, direction)
                child = norm((at[0] + step[0], at[1] + step[1]))
                parent[child] = (at, step)
                at = child

    root = (0, 0)
    if part == 0:
        ring(root, 1, NY, 1)
        for ny in range(NY):
            ring((0, ny), 0, NZ, 1 if ny % 2 == 0 else -1)
    else:
        ring(root, 0, NZ, -1)
        for nz in range(NZ):
            ring((nz, 0), 1, NY, -1 if nz % 2 == 0 else 1)
    return parent


TREES = (make_tree(0), make_tree(1))
CHILDREN = []
DEPTH = []
HEIGHT = []
for tree in TREES:
    kids = {}
    for child, (par, step) in tree.items():
        kids.setdefault(par, []).append((child, step))
    depth = {(0, 0): 0}
    todo = [(0, 0)]
    order = []
    while todo:
        at = todo.pop(0)
        order.append(at)
        for child, _ in kids.get(at, []):
            depth[child] = depth[at] + 1
            todo.append(child)
    height = {}
    for at in reversed(order):
        height[at] = max([1 + height[c] for c, _ in kids.get(at, [])], default=0)
    for at in kids:
        kids[at].sort(key=lambda item: -height[item[0]])
    CHILDREN.append(kids)
    DEPTH.append(depth)
    HEIGHT.append(height)

EDGES = [(p, n) for p in (0, 1) for n in sorted(TREES[p])]
EDGE_ID = {edge: i for i, edge in enumerate(EDGES)}
LINK_US = [rows * CH * 2 * 2 / 90e3 for _, rows in ROWS]
HOP_US = 1.7


def plan_gather():
    free, arrivals, events = {}, [], []
    state = {"t": 0.0}

    def forward(p, n):
        for child, step in CHILDREN[p].get(n, []):
            begin = max(state["t"], free.get(step, 0.0))
            free[step] = begin + LINK_US[p]
            heapq.heappush(arrivals, (free[step] + HOP_US, p, child))

    for p in (1, 0):
        forward(p, (0, 0))
    seen = {}
    ready = [(0, 0)]
    done = 0
    while arrivals or ready:
        if arrivals and arrivals[0][0] <= state["t"]:
            _, p, n = heapq.heappop(arrivals)
            events.append(("recv", p, n))
            state["t"] += 0.05
            forward(p, n)
            seen[n] = seen.get(n, 0) + 1
            if seen[n] == 2:
                ready.append(n)
        elif ready:
            n = ready.pop(0)
            events.append(("comp", n))
            state["t"] += 0.45
            done += 1
        else:
            state["t"] = arrivals[0][0]
    return events, state["t"]


def plan_reduce():
    free, arrivals, order = {}, [], []
    t = 0.0
    missing = {(p, n): len(CHILDREN[p].get(n, [])) for p in (0, 1) for n in list(TREES[p]) + [(0, 0)]}
    ready = [key for key, count in missing.items() if count == 0]
    while arrivals or ready:
        while arrivals and arrivals[0][0] <= t:
            _, p, n = heapq.heappop(arrivals)
            missing[(p, n)] -= 1
            if missing[(p, n)] == 0:
                ready.append((p, n))

        def key(item):
            p, n = item
            if n == (0, 0):
                return (2, 0.0)
            backlog = free.get(TREES[p][n][1], 0.0) - t
            return (0 if backlog < 2.5 else 1, -DEPTH[p][n], backlog)

        ready.sort(key=key)
        if ready and (key(ready[0])[0] == 0 or not arrivals or key(ready[0])[0] == 2):
            p, n = ready.pop(0)
            order.append((p, n))
            t += 0.3
            if n != (0, 0):
                par, step = TREES[p][n]
                begin = max(t, free.get(step, 0.0))
                free[step] = begin + LINK_US[p]
                heapq.heappush(arrivals, (free[step] + HOP_US, p, par))
        else:
            nexts = [arrivals[0][0]] if arrivals else []
            if ready:
                nexts.append(t + 0.2)
            t = min(nexts)
    return order, t


GATHER, GATHER_US = plan_gather()
REDUCE, REDUCE_US = plan_reduce()


def rope_table(length):
    half = HD // 2
    inverse = np.exp(np.arange(half) * (-2.0 * math.log(rope_base) / HD))
    angles = np.arange(length)[:, None] * inverse[None, :]
    return np.concatenate([np.cos(angles), np.sin(angles)], axis=1).astype(np.float32)


def dot(a, b):
    return jnp.dot(a, b, preferred_element_type=F32)


def dot_nt(a, b, precision=None):
    return lax.dot_general(a, b, (((1,), (1,)), ((), ())), preferred_element_type=F32, precision=precision)


def kernel(
    act, gain, wq_h, kv_h, wo_h, ids, clean, rope_h, out,
    xg, held, wq, kvraw, wo, rope, perm, acc_m, acc_o, orecv, qbuf, kv, num, den, att, sbuf, rbuf,
    sqz, sqy, sqs,
    g_send, g_recv, r_send, r_recv, s_send, s_recv, x_send, x_recv, c_send, c_recv, load_sem,
):
    col = lax.axis_index("col")
    row = lax.axis_index("row")
    seq = lax.axis_index("seq")
    z, y = col // NY, lax.rem(col, NY)
    other = 1 - row

    def plane(step):
        zz = lax.rem(z + step[0] + NZ, NZ)
        yy = lax.rem(y + step[1] + NY, NY)
        return {"col": zz * NY + yy}

    def origin(n):
        return lax.rem(z + NZ - n[0] % NZ, NZ) * NY + lax.rem(y + NY - n[1] % NY, NY)

    def along(step):
        return {"seq": lax.rem(seq + step + 4, 4)}

    sibling = {"row": other}

    barrier = pltpu.get_barrier_semaphore()
    partners = [plane(s) for s in ((1, 0), (-1, 0), (0, 1), (0, -1))] + [along(1), along(-1), sibling]
    for device in partners:
        pl.semaphore_signal(barrier, inc=1, device_id=device, device_id_type=MESH)

    def dyn(index, size):
        return pl.ds(pl.multiple_of(index * size, size), size)

    group = col // 8
    loads = [
        pltpu.make_async_copy(wq_h.at[:, dyn(row, HD)], wq.at[:, pl.ds(0, HD)], load_sem.at[0]),
        pltpu.make_async_copy(wq_h.at[:, dyn(other, HD)], wq.at[:, pl.ds(HD, HD)], load_sem.at[1]),
        pltpu.make_async_copy(kv_h.at[:, :, dyn(group, HD)], kvraw, load_sem.at[2]),
        pltpu.make_async_copy(rope_h.at[dyn(seq, SLAB), :], rope, load_sem.at[3]),
        pltpu.make_async_copy(wo_h.at[dyn(row, HD), :], wo.at[pl.ds(0, HD), :], load_sem.at[4]),
        pltpu.make_async_copy(wo_h.at[dyn(other, HD), :], wo.at[pl.ds(HD, HD), :], load_sem.at[5]),
    ]
    for copy in loads:
        copy.start()

    wide = act[...].astype(F32)
    xg[...] = (wide * gain[...]).astype(BF16)
    pl.semaphore_wait(barrier, len(partners))

    sent = []

    def remote(src, dst, send, recv, device):
        return pltpu.make_async_remote_copy(
            src_ref=src, dst_ref=dst, send_sem=send, recv_sem=recv, device_id=device, device_id_type=MESH
        )

    def launch(copy):
        copy.start()
        sent.append(copy)

    def chunk(n, p):
        first, rows = ROWS[p]
        if n == (0, 0):
            return xg.at[pl.ds(first, rows), :]
        return held.at[slot(n), pl.ds(first, rows), :]

    def gather_copy(p, n, child, step):
        e = EDGE_ID[(p, child)]
        return remote(chunk(n, p), chunk(child, p), g_send.at[e], g_recv.at[e], plane(step))

    def forward(p, n):
        for child, step in CHILDREN[p].get(n, []):
            launch(gather_copy(p, n, child, step))

    forward(1, (0, 0))
    forward(0, (0, 0))

    ones = jnp.ones((8, CH), F32)
    sqz[0] = dot_nt(ones, wide * wide, lax.Precision.HIGHEST)

    def sqz_forward(nz):
        for child, step in CHILDREN[1].get((nz, 0), []):
            if step[0]:
                k = child[0]
                launch(remote(sqz.at[nz], sqz.at[k], s_send.at[k], s_recv.at[k], plane(step)))

    def sqy_forward(ny):
        for child, step in CHILDREN[0].get((0, ny), []):
            if step[1]:
                k = child[1]
                launch(remote(sqy.at[ny], sqy.at[k], s_send.at[8 + k], s_recv.at[8 + k], plane(step)))

    def landed(dst, recv, device):
        remote(dst, dst, recv, recv, device).wait_recv()

    sqz_forward(0)

    line = lax.broadcasted_iota(jnp.int32, (2 * CH, 2 * CH), 0)
    lane = lax.broadcasted_iota(jnp.int32, (2 * CH, 2 * CH), 1)
    upper = (line >= CH).astype(jnp.int32)
    kind = jnp.where(row == 0, upper, 1 - upper)
    perm[...] = jnp.where(lane == 2 * (line - CH * upper) + kind, 1.0, 0.0).astype(BF16)
    acc_m[...] = jnp.zeros_like(acc_m)
    acc_o[...] = jnp.zeros_like(acc_o)
    for copy in loads[:4]:
        copy.wait()

    def compute(n):
        at = origin(n)
        wrow = dyn(at, CH)
        pairs = kvraw[wrow, :, :].reshape(2 * CH, HD)
        split = dot(perm[...], pairs).astype(BF16)
        mine = jnp.concatenate([wq[wrow, pl.ds(0, HD)], split[:CH]], axis=1)
        theirs = jnp.concatenate([wq[wrow, pl.ds(HD, HD)], split[CH:]], axis=1)
        x = xg[...] if n == (0, 0) else held[slot(n)]
        acc_m[...] += dot(x, mine)
        acc_o[...] += dot(x, theirs)

    z_left = NZ - 1
    events = list(GATHER)
    for position, event in enumerate(events):
        if event[0] == "comp":
            compute(event[1])
            continue
        _, p, n = event
        step = TREES[p][n][1]
        e = EDGE_ID[(p, n)]
        landed(chunk(n, p), g_recv.at[e], plane((-step[0], -step[1])))
        forward(p, n)
        if p == 1 and n[1] == 0:
            landed(sqz.at[n[0]], s_recv.at[n[0]], plane((-step[0], -step[1])))
            sqz_forward(n[0])
            z_left -= 1
            if z_left == 0:
                total = sqz[0]
                for k in range(1, NZ):
                    total = total + sqz[k]
                sqy[0] = total
                sqy_forward(0)
        if position == len(events) - 16:
            landed(sqy.at[1], s_recv.at[9], plane((0, -1)))
            sqy_forward(1)
        if position == len(events) - 4:
            pass

    launch(remote(acc_o, orecv, c_send.at[0], c_recv.at[0], sibling))
    landed(sqy.at[2], s_recv.at[10], plane((0, -1)))
    landed(sqy.at[3], s_recv.at[11], plane((0, 1)))
    sqs[0] = sqy[0] + sqy[1] + sqy[2] + sqy[3]
    launch(remote(sqs.at[0], sqs.at[1], c_send.at[1], c_recv.at[1], sibling))

    table = rope[...]
    turned = pltpu.roll(table, HD // 2, 1)
    low = lax.broadcasted_iota(jnp.int32, (SLAB, HD), 1) < HD // 2
    cosine = jnp.where(low, table, turned)
    sine = jnp.where(low, -turned, table)
    is_key = (row == 0).astype(F32)
    cos_kv = cosine * is_key + (1.0 - is_key)
    sin_kv = sine * is_key

    landed(sqs.at[1], c_recv.at[1], sibling)
    squares = sqs[0] + sqs[1]
    scaling = lax.rsqrt(squares[:1] / D + norm_eps)
    scale_col = jnp.broadcast_to(scaling, (HD, SLAB)).T
    my_ids = ids[:, dyn(seq, SLAB)].astype(F32)
    own = jnp.broadcast_to(my_ids, (HD, SLAB)).T

    landed(orecv, c_recv.at[0], sibling)
    kv_sum = (acc_m[:, HD:] + orecv[:, HD:]) * scale_col
    kv[row, 0] = (kv_sum * cos_kv + pltpu.roll(kv_sum, HD // 2, 1) * sin_kv).astype(BF16)

    half = SLAB // 2
    launch(remote(kv.at[row, 0], kv.at[row, 1], x_send.at[0], x_recv.at[0], along(1)))
    launch(remote(kv.at[row, 0], kv.at[row, 3], x_send.at[1], x_recv.at[1], along(-1)))
    launch(remote(kv.at[row, 0], kv.at[row, 0], c_send.at[2], c_recv.at[2], sibling))

    q_sum = (acc_m[:, :HD] + orecv[:, :HD]) * scale_col
    qbuf[...] = (q_sum * cosine + pltpu.roll(q_sum, HD // 2, 1) * sine).astype(BF16)
    num[...] = jnp.zeros_like(num)
    den[...] = jnp.zeros_like(den)
    score_scale = 1.0 / math.sqrt(HD)

    own_ids = own

    def attend(k):
        from_seq = lax.rem(seq + 4 - k, 4)
        key_ids = ids[:, dyn(from_seq, SLAB)].astype(F32)
        open_to = jnp.where(clean[:, dyn(from_seq, SLAB)] == 1, 1e9, key_ids)
        scores = dot_nt(qbuf[...], kv[0, k]) * score_scale
        mine = own_ids[:, :1]
        visible = (mine >= key_ids) & (mine <= open_to)
        weights = jnp.where(visible, jnp.exp(scores), 0.0)
        den[...] += weights[:, 0:128] + weights[:, 128:256] + weights[:, 256:384] + weights[:, 384:512]
        num[...] += dot(weights.astype(BF16), kv[1, k])

    landed(kv.at[other, 0], c_recv.at[2], sibling)
    landed(kv.at[row, 1], x_recv.at[0], along(-1))
    launch(remote(kv.at[row, 1, pl.ds(0, half)], kv.at[row, 2, pl.ds(0, half)], x_send.at[2], x_recv.at[2], along(1)))
    launch(remote(kv.at[row, 1], kv.at[row, 1], c_send.at[3], c_recv.at[3], sibling))
    landed(kv.at[row, 3], x_recv.at[1], along(1))
    launch(
        remote(kv.at[row, 3, pl.ds(half, half)], kv.at[row, 2, pl.ds(half, half)], x_send.at[3], x_recv.at[3], along(-1))
    )
    launch(remote(kv.at[row, 3], kv.at[row, 3], c_send.at[4], c_recv.at[4], sibling))
    attend(0)
    landed(kv.at[row, 2, pl.ds(0, half)], x_recv.at[2], along(-1))
    landed(kv.at[row, 2, pl.ds(half, half)], x_recv.at[3], along(1))
    launch(remote(kv.at[row, 2], kv.at[row, 2], c_send.at[5], c_recv.at[5], sibling))
    landed(kv.at[other, 1], c_recv.at[3], sibling)
    attend(1)
    landed(kv.at[other, 3], c_recv.at[4], sibling)
    attend(3)
    landed(kv.at[other, 2], c_recv.at[5], sibling)
    attend(2)

    att[0] = (num[...] / jnp.sum(den[...], axis=1, keepdims=True)).astype(BF16)
    launch(remote(att.at[0], att.at[1], c_send.at[6], c_recv.at[6], sibling))
    for copy in loads[4:]:
        copy.wait()
    landed(att.at[1], c_recv.at[6], sibling)

    for p, n in REDUCE:
        first, rows = ROWS[p]
        block = pl.ds(first, rows)
        left = jnp.concatenate([att[0, block, :], att[1, block, :]], axis=1)
        value = dot(left, wo[:, dyn(origin(n), CH)])
        for child, step in CHILDREN[p].get(n, []):
            e = EDGE_ID[(p, child)]
            landed(rbuf.at[slot(child), block, :], r_recv.at[e], plane(step))
            value = value + rbuf[slot(child), block, :].astype(F32)
        if n == (0, 0):
            out[block, :] = value.astype(BF16)
            continue
        e = EDGE_ID[(p, n)]
        step = TREES[p][n][1]
        sbuf[slot(n), block, :] = value.astype(BF16)
        launch(
            remote(
                sbuf.at[slot(n), block, :], rbuf.at[slot(n), block, :],
                r_send.at[e], r_recv.at[e], plane((-step[0], -step[1])),
            )
        )

    for copy in sent:
        copy.wait_send()


def shards(activations, norm_gain, query_weight, kv_weight, out_weight, block_ids, clean_mask):
    features = query_weight.shape[0]
    length = block_ids.shape[0]
    vmem = pl.BlockSpec(memory_space=pltpu.VMEM)
    hbm = pl.BlockSpec(memory_space=pl.ANY)
    dma = pltpu.SemaphoreType.DMA
    edges = len(EDGES)
    return pl.pallas_call(
        kernel,
        out_shape=jax.ShapeDtypeStruct((SLAB, CH), BF16),
        in_specs=[vmem, vmem, hbm, hbm, hbm, vmem, vmem, hbm],
        out_specs=vmem,
        scratch_shapes=[
            pltpu.VMEM((SLAB, CH), BF16),
            pltpu.VMEM((NZ * NY, SLAB, CH), BF16),
            pltpu.VMEM((features, 2 * HD), BF16),
            pltpu.VMEM((features, 2, HD), BF16),
            pltpu.VMEM((2 * HD, out_weight.shape[1]), BF16),
            pltpu.VMEM((SLAB, HD), F32),
            pltpu.VMEM((2 * CH, 2 * CH), BF16),
            pltpu.VMEM((SLAB, 2 * HD), F32),
            pltpu.VMEM((SLAB, 2 * HD), F32),
            pltpu.VMEM((SLAB, 2 * HD), F32),
            pltpu.VMEM((SLAB, HD), BF16),
            pltpu.VMEM((2, 4, SLAB, HD), BF16),
            pltpu.VMEM((SLAB, HD), F32),
            pltpu.VMEM((SLAB, HD), F32),
            pltpu.VMEM((2, SLAB, HD), BF16),
            pltpu.VMEM((NZ * NY, SLAB, CH), BF16),
            pltpu.VMEM((NZ * NY, SLAB, CH), BF16),
            pltpu.VMEM((NZ, 8, SLAB), F32),
            pltpu.VMEM((NY, 8, SLAB), F32),
            pltpu.VMEM((2, 8, SLAB), F32),
            dma((edges,)), dma((edges,)), dma((edges,)), dma((edges,)),
            dma((12,)), dma((12,)), dma((4,)), dma((4,)), dma((7,)), dma((7,)), dma((6,)),
        ],
        compiler_params=pltpu.CompilerParams(
            collective_id=0, has_side_effects=True, vmem_limit_bytes=63 * 1024 * 1024
        ),
        name="layer",
    )(
        activations,
        norm_gain.reshape(1, CH),
        query_weight,
        kv_weight,
        out_weight,
        block_ids.reshape(1, length),
        clean_mask.reshape(1, length),
        jnp.asarray(rope_table(length)),
    )


def solution(mesh):
    placed = (
        P("seq", ("row", "col")),
        P(("row", "col")),
        P("row", "col"),
        P("row", None, None),
        P("col", "row"),
        P(),
        P(),
    )
    return jax.shard_map(
        shards, mesh=mesh, in_specs=placed, out_specs=P("seq", ("row", "col")), check_vma=False
    )
```

time: 590 us -> 127 us (0.22)
  waiting for transfers between devices: 367 us -> 0 us
  blocking collectives: 161 us -> 0 us
  Pallas kernels: 0 us -> 125 us
  matrix products: 25.3 us -> 0 us
  between operations: 13.2 us -> 0.01 us
  local copies, waits for them, and re-layouts: 10.5 us -> 1.67 us
  other arithmetic: 8.15 us -> 0 us
    reduce_scatter x2 -> x0, waiting for transfers between devices: 245 us -> none  [the longest x1 245 us: shards(): lax.psum_scatter(partial_out, 'col', scatter_dimension=1, tiled=True)]
    psum x1 -> x0, blocking collectives: 133 us -> none  [shards(): squares = lax.psum(jnp.sum(wide_input * wide_input, axis=1), ('row', 'col'))]
    pallas_call x0 -> x1, Pallas kernels: none -> 125 us  [shards(): pl.pallas_call(kernel, out_shape=jax.ShapeDtypeStruct((SLAB, CH), BF16),...]
    all_gather x1 -> x0, waiting for transfers between devices: 98.1 us -> none  [shards(): panel_rows = lax.all_gather(normed, 'col', axis=1, tiled=True)]
    all_gather x3 -> x0, blocking collectives: 27.8 us -> none  [the longest x1 10.7 us: shards(): key_piece = lax.all_gather(key_rows, 'seq', axis=0, tiled=True)]
    dot_general x5 -> x0, matrix products: 25.3 us -> none  [the longest x1 7.87 us: shards(): jnp.einsum('td,dke->kte', panel_rows, kv_tiles, preferred_element_type=jn...]
    psum x1 -> x0, waiting for transfers between devices: 24.3 us -> none  [shards(): kv_sum = lax.psum(kv_term, 'row')]
    dynamic_slice x2 -> x0, local copies, waits for them, and re-layouts: 8.54 us -> none  [the longest x1 7.78 us: shards(): lax.dynamic_slice_in_dim(kv_weight, kv_first * HD, kv_count * HD, 2)]
  transfers between devices with their start and end apart: 4 -> 0, of which waited for: 3 -> 0; matrix products, arithmetic and copies ran while one was open for 3% -> 0% of each run, Pallas kernels for 0% -> 0%
where the time goes in v1:
time: 127 us
  Pallas kernels  125 us (98%)
  local copies, waits for them, and re-layouts  1.67 us (1%)
    pallas_call x1, Pallas kernels, shards(): pl.pallas_call(kernel, out_shape=jax.ShapeDtypeStruct((SLAB, CH), BF16),...  125 us

profile of v1, /device:TPU:1, one launch (start us, length us, event | category | flops | bytes accessed | tf_op | source)
XLA Modules:
  0.0 127.0 jit_solution(8344429864604674683)
XLA Ops:
  0.0 125.3 %layer.1 = bf16[512,256]{1,0:T(8,128)(2,1)} custom-call(bf16[512,256]{1,0:T(8,128)(2,1)} %act.1, f32[1,256]{1,0:T(1,128)} %bitcast.5, bf16[8192,256]{1,0:T(8,128)(2,1)} %wq_h.1, bf16[8192,2,512]{2,1,0:T(2,128)(2,1)} %kv_h.1, bf16[256,8192]{1,0:T(8,128)(2,1)} %wo_h.1, s32[1,2048]{1,0:T(1,128)} %bitcast.3, s32[1,2048]{1,0:T(1,128)} %bitcast.4, ...), custom_call_target="tpu_custom_call" | custom-call | tf_op jit(solution)/shard_map/layer/pallas_call | solution.py:438
  125.3 1.7 %copy.10 = bf16[512,256]{1,0:T(8,128)(2,1)} copy(bf16[512,256]{1,0:T(8,128)(2,1)} %layer.1) | data formatting | bytes 524288

commit v2 on v1

v2 whole, which is shorter than its diff:
```python
import heapq
import math
import random

import jax
import jax.numpy as jnp
import numpy as np
from jax import lax
from jax.experimental import pallas as pl
from jax.experimental.pallas import tpu as pltpu
from jax.sharding import PartitionSpec as P

D = 16384
HD = 128
QH = 64
KVH = 4
rope_base = 500000.0
norm_eps = 1e-05

MESH = pl.DeviceIdType.MESH
VMEM_LIMIT = 63 * 1024 * 1024
F32 = jnp.float32
BF16 = jnp.bfloat16

NZ, NY = 8, 4
SLAB = 512
SPLIT = 208
PARTS = ((0, SPLIT, True), (SPLIT, SLAB - SPLIT, False))
ROWS = tuple(part[:2] for part in PARTS)
CH = 256


def norm(n):
    return (n[0] % NZ, n[1] % NY)


def slot(n):
    return (n[0] % NZ) * NY + n[1] % NY


HOP_US = 1.7
COMP_US = 0.3
LOADED_US = 8.0
HALVED = True

HALVES = tuple(
    (slice(first, first + (rows // 32 + rows % 32 // 16) * 16), slice(first + (rows // 32 + rows % 32 // 16) * 16, first + rows))
    for first, rows in ROWS
)
WHOLE = tuple(slice(first, first + rows) for first, rows in ROWS)


def make_tree(part, y_first):
    edges = []

    def ring(start, axis, size, way, halved):
        for direction, hops in ((way, size // 2), (-way, size // 2 - 1)):
            at = start
            for hop in range(1, size // 2 + 1):
                step = (direction, 0) if axis == 0 else (0, direction)
                child = norm((at[0] + step[0], at[1] + step[1]))
                far = hop == size // 2
                if far and halved:
                    edges.append((at, child, step, HALVES[part][direction == way]))
                elif hop <= hops:
                    edges.append((at, child, step, WHOLE[part]))
                at = child

    root = (0, 0)
    if y_first:
        ring(root, 1, NY, 1, HALVED)
        for ny in range(NY):
            ring((0, ny), 0, NZ, 1 if ny % 2 == 0 else -1, False)
    else:
        ring(root, 0, NZ, -1, HALVED)
        for nz in range(NZ):
            ring((nz, 0), 1, NY, -1 if nz % 2 == 0 else 1, False)
    return edges


EDGES = [(part,) + edge for part, spec in enumerate(PARTS) for edge in make_tree(part, spec[2])]
DOWN, UP = {}, {}
for number, edge in enumerate(EDGES):
    DOWN.setdefault((edge[0], edge[1]), []).append(number)
    UP.setdefault((edge[0], edge[2]), []).append(number)
NODES = [(part, (nz, ny)) for part in range(len(PARTS)) for nz in range(NZ) for ny in range(NY)]


def height(key):
    return max([1 + height((key[0], EDGES[e][2])) for e in DOWN.get(key, [])], default=0)


def depth(key):
    return max([1 + depth((key[0], EDGES[e][1])) for e in UP.get(key, [])], default=0)


DEPTH = {key: depth(key) for key in NODES}
for key in DOWN:
    DOWN[key].sort(key=lambda e: -height((EDGES[e][0], EDGES[e][2])))


def link_us(e):
    rows = EDGES[e][4]
    return (rows.stop - rows.start) * CH * 2 * 2 / 95e3


def tail_down(key):
    return max([link_us(e) + HOP_US + tail_down((key[0], EDGES[e][2])) for e in DOWN.get(key, [])], default=0.0)


def tail_up(key):
    return max([link_us(e) + HOP_US + 0.3 + tail_up((key[0], EDGES[e][1])) for e in UP.get(key, [])], default=0.0)


def plan_gather(backlog=1.0):
    rank = [tail_down((edge[0], edge[2])) for edge in EDGES]
    free, arrivals, events = {}, [], []
    pending = [e for part in (0, 1) for e in DOWN[(part, (0, 0))]]
    missing = {key: len(UP.get(key, [])) for key in NODES}
    ready = [(0, (0, 0)), (1, (0, 0))]
    t = 0.0
    while arrivals or ready or pending:
        able = [e for e in pending if free.get(EDGES[e][3], 0.0) - t < backlog]
        if able:
            e = max(able, key=lambda e: rank[e])
            pending.remove(e)
            step = EDGES[e][3]
            free[step] = max(t, free.get(step, 0.0)) + link_us(e)
            heapq.heappush(arrivals, (free[step] + HOP_US, e))
            events.append(("send", e))
            t += 0.01
        elif arrivals and arrivals[0][0] <= t:
            _, e = heapq.heappop(arrivals)
            events.append(("recv", e))
            t += 0.04
            key = (EDGES[e][0], EDGES[e][2])
            missing[key] -= 1
            if missing[key] == 0:
                pending += DOWN.get(key, [])
                ready.append(key)
        elif ready and t >= LOADED_US:
            events.append(("comp",) + ready.pop(0))
            t += COMP_US
        else:
            nexts = [arrivals[0][0]] if arrivals else []
            if t < LOADED_US:
                nexts.append(LOADED_US)
            if pending:
                nexts.append(min(free[EDGES[e][3]] for e in pending) - backlog + 0.001)
            t = max(t + 0.001, min(nexts))
    return events, t


def plan_reduce(backlog=2.0, jitter=0.5, seed=1):
    draw = random.Random(seed)
    rank = {key: tail_up(key) + jitter * draw.random() for key in NODES}
    free, arrivals, order = {}, [], []
    missing = {key: len(DOWN.get(key, [])) for key in NODES}
    ready = [key for key in NODES if missing[key] == 0]
    t = 0.0

    def behind(key):
        return max(free.get(EDGES[e][3], 0.0) for e in UP[key]) - t

    while arrivals or ready:
        while arrivals and arrivals[0][0] <= t:
            _, e = heapq.heappop(arrivals)
            above = (EDGES[e][0], EDGES[e][1])
            missing[above] -= 1
            if missing[above] == 0:
                ready.append(above)
        able = [key for key in ready if key in UP and behind(key) < backlog]
        roots = [key for key in ready if key not in UP]
        if able:
            key = max(able, key=lambda key: rank[key] - 0.5 * max(0.0, behind(key)))
        elif roots:
            key = roots[0]
        else:
            nexts = [arrivals[0][0]] if arrivals else []
            if ready:
                nexts.append(min(behind(key) for key in ready) + t - backlog + 0.001)
            t = max(t + 0.001, min(nexts))
            continue
        ready.remove(key)
        order.append(key)
        t += 0.1 + 0.2 * ROWS[key[0]][1] / CH
        for e in UP.get(key, []):
            step = EDGES[e][3]
            free[step] = max(t, free.get(step, 0.0)) + link_us(e)
            heapq.heappush(arrivals, (free[step] + HOP_US, e))
    return order, t


GATHER, GATHER_US = plan_gather()
REDUCE, REDUCE_US = plan_reduce()
RECVS = [i for i, event in enumerate(GATHER) if event[0] == "recv"]
FIRST_AT, SQUARES_AT = RECVS[4], (RECVS[-18], RECVS[-11], RECVS[-5])


def rope_tables():
    half = HD // 2
    inverse = np.exp(np.arange(half) * (-2.0 * math.log(rope_base) / HD))
    angles = np.arange(SLAB)[:, None] * inverse[None, :]
    within = np.concatenate([np.cos(angles), np.sin(angles)], axis=1)
    starts = np.tile(np.arange(4)[:, None] * SLAB * inverse[None, :], (1, 2))
    return within.astype(np.float32), np.concatenate([np.cos(starts), np.sin(starts)]).astype(np.float32)


def dot(a, b):
    return jnp.dot(a, b, preferred_element_type=F32)


def dot_nt(a, b, precision=None):
    return lax.dot_general(a, b, (((1,), (1,)), ((), ())), preferred_element_type=F32, precision=precision)


def kernel(
    act_h, gain_h, wq_h, kv_h, wo_h, ids_h, clean_h, within_h, starts_h, out,
    act, gain, ids, clean, within, starts,
    xg, held, wq, kvraw, wkv, wo, perm, cosine, sine, scale_col, own_ids,
    accq_m, acckv_m, accq_o, acckv_o, recvq, recvkv, qbuf, kv, num, den, att, sbuf, rbuf,
    sqz, sqy, sqs,
    g_send, g_recv, r_send, r_recv, s_send, s_recv, x_send, x_recv, c_send, c_recv, load_sem,
):
    col = lax.axis_index("col")
    row = lax.axis_index("row")
    seq = lax.axis_index("seq")
    z, y = col // NY, lax.rem(col, NY)
    other = 1 - row

    def plane(step):
        zz = lax.rem(z + step[0] + NZ, NZ)
        yy = lax.rem(y + step[1] + NY, NY)
        return {"col": zz * NY + yy}

    def origin(n):
        return lax.rem(z + NZ - n[0] % NZ, NZ) * NY + lax.rem(y + NY - n[1] % NY, NY)

    def along(step):
        return {"seq": lax.rem(seq + step + 4, 4)}

    sibling = {"row": other}

    barrier = pltpu.get_barrier_semaphore()
    partners = [plane(s) for s in ((1, 0), (-1, 0), (0, 1), (0, -1))] + [along(1), along(-1), sibling]
    for device in partners:
        pl.semaphore_signal(barrier, inc=1, device_id=device, device_id_type=MESH)

    def dyn(index, size):
        return pl.ds(pl.multiple_of(index * size, size), size)

    group = col // 8
    pieces = (
        (act_h, act),
        (gain_h, gain),
        (kv_h.at[:, :, dyn(group, HD)], kvraw),
        (wq_h.at[:, dyn(row, HD)], wq.at[:, pl.ds(0, HD)]),
        (wq_h.at[:, dyn(other, HD)], wq.at[:, pl.ds(HD, HD)]),
        (within_h, within),
        (starts_h, starts),
        (ids_h, ids),
        (clean_h, clean),
        (wo_h.at[dyn(row, HD), :], wo.at[pl.ds(0, HD), :]),
        (wo_h.at[dyn(other, HD), :], wo.at[pl.ds(HD, HD), :]),
    )
    loads = [pltpu.make_async_copy(src, dst, load_sem.at[i]) for i, (src, dst) in enumerate(pieces)]
    for copy in loads:
        copy.start()
    loads[0].wait()
    loads[1].wait()
    wide = act[...].astype(F32)
    xg[...] = (wide * gain[...]).astype(BF16)
    pl.semaphore_wait(barrier, len(partners))

    sent = []

    def remote(src, dst, send, recv, device):
        return pltpu.make_async_remote_copy(
            src_ref=src, dst_ref=dst, send_sem=send, recv_sem=recv, device_id=device, device_id_type=MESH
        )

    def launch(copy):
        copy.start()
        sent.append(copy)

    def landed(dst, recv, device):
        remote(dst, dst, recv, recv, device).wait_recv()

    def chunk(n, rows):
        block = pl.ds(rows.start, rows.stop - rows.start)
        if n == (0, 0):
            return xg.at[block, :]
        return held.at[slot(n), block, :]

    def send(e):
        _, above, below, step, rows = EDGES[e]
        launch(remote(chunk(above, rows), chunk(below, rows), g_send.at[e], g_recv.at[e], plane(step)))

    own_sends = next(i for i, event in enumerate(GATHER) if event[0] != "send")
    for event in GATHER[:own_sends]:
        send(event[1])

    sqz[0] = dot_nt(jnp.ones((8, CH), F32), wide * wide, lax.Precision.HIGHEST)

    def square_ring(ref, at, axis, base):
        size = ref.shape[0]
        for direction, hops in ((1, size // 2), (-1, size // 2 - 1)):
            distance = at if direction == 1 else (size - at) % size
            if distance < hops and (at == 0 or distance < size // 2):
                k = (at + direction) % size
                step = (direction, 0) if axis == 0 else (0, direction)
                launch(remote(ref.at[at], ref.at[k], s_send.at[base + k], s_recv.at[base + k], plane(step)))

    def sqz_forward(nz):
        square_ring(sqz, nz, 0, 0)

    def sqy_forward(ny):
        square_ring(sqy, ny, 1, 8)

    sqz_forward(0)

    line = lax.broadcasted_iota(jnp.int32, (2 * CH, 2 * CH), 0)
    lane = lax.broadcasted_iota(jnp.int32, (2 * CH, 2 * CH), 1)
    upper = (line >= CH).astype(jnp.int32)
    kind = jnp.where(row == 0, upper, 1 - upper)
    perm[...] = jnp.where(lane == 2 * (line - CH * upper) + kind, 1.0, 0.0).astype(BF16)
    for acc in (accq_m, acckv_m, accq_o, acckv_o):
        acc[...] = jnp.zeros_like(acc)

    apart = set()

    def compute(pair, n):
        if not apart:
            for copy in loads[2:5]:
                copy.wait()
        at = dyn(origin(n), CH)
        if n not in apart:
            apart.add(n)
            split = dot(perm[...], kvraw[at, :, :].reshape(2 * CH, HD)).astype(BF16)
            wkv[at, pl.ds(0, HD)] = split[:CH]
            wkv[at, pl.ds(HD, HD)] = split[CH:]
        first, rows = ROWS[pair]
        block = pl.ds(first, rows)
        x = xg[block, :] if n == (0, 0) else held[slot(n), block, :]
        theirs = dot(x, jnp.concatenate([wkv[at, pl.ds(HD, HD)], wq[at, pl.ds(HD, HD)]], axis=1))
        acckv_o[block, :] += theirs[:, :HD]
        accq_o[block, :] += theirs[:, HD:]
        mine = dot(x, jnp.concatenate([wkv[at, pl.ds(0, HD)], wq[at, pl.ds(0, HD)]], axis=1))
        acckv_m[block, :] += mine[:, :HD]
        accq_m[block, :] += mine[:, HD:]

    def prepare():
        for copy in loads[5:9]:
            copy.wait()
        table = within[...]
        turned = pltpu.roll(table, HD // 2, 1)
        low = lax.broadcasted_iota(jnp.int32, (SLAB, HD), 1) < HD // 2
        cos_t, sin_t = jnp.where(low, table, turned), jnp.where(low, turned, table)
        cos_s, sin_s = starts[pl.ds(seq, 1), :], starts[pl.ds(seq + 4, 1), :]
        cosine[...] = cos_t * cos_s - sin_t * sin_s
        both = sin_t * cos_s + cos_t * sin_s
        sine[...] = jnp.where(low, -both, both)
        own_ids[...] = jnp.broadcast_to(ids[:, dyn(seq, SLAB)].astype(F32), (HD, SLAB)).T
        num[...] = jnp.zeros_like(num)
        den[...] = jnp.zeros_like(den)

    z_left = NZ - 1
    missing = {key: len(UP.get(key, [])) for key in NODES}
    for position, event in enumerate(GATHER):
        if position < own_sends:
            continue
        if position == FIRST_AT:
            prepare()
        if position == SQUARES_AT[0]:
            landed(sqy.at[1], s_recv.at[9], plane((0, -1)))
            sqy_forward(1)
        if position == SQUARES_AT[1]:
            landed(sqy.at[2], s_recv.at[10], plane((0, -1)))
            landed(sqy.at[3], s_recv.at[11], plane((0, 1)))
            sqs[0] = sqy[0] + sqy[1] + sqy[2] + sqy[3]
            launch(remote(sqs.at[0], sqs.at[1], c_send.at[1], c_recv.at[1], sibling))
        if position == SQUARES_AT[2]:
            landed(sqs.at[1], c_recv.at[1], sibling)
            squares = sqs[0] + sqs[1]
            scaling = lax.rsqrt(squares[:1] / D + norm_eps)
            scale_col[...] = jnp.broadcast_to(scaling, (HD, SLAB)).T
        if event[0] == "comp":
            compute(event[1], event[2])
            continue
        if event[0] == "send":
            send(event[1])
            continue
        part, above, n, step, rows = EDGES[event[1]]
        landed(chunk(n, rows), g_recv.at[event[1]], plane((-step[0], -step[1])))
        missing[(part, n)] -= 1
        if missing[(part, n)]:
            continue
        if part == 1 and n[1] == 0:
            landed(sqz.at[n[0]], s_recv.at[n[0]], plane((-1, 0) if n[0] <= NZ // 2 else (1, 0)))
            sqz_forward(n[0])
            z_left -= 1
            if z_left == 0:
                total = sqz[0]
                for k in range(1, NZ):
                    total = total + sqz[k]
                sqy[0] = total
                sqy_forward(0)

    launch(remote(acckv_o, recvkv, c_send.at[0], c_recv.at[0], sibling))
    launch(remote(accq_o, recvq, c_send.at[7], c_recv.at[7], sibling))

    half = SLAB // 2
    halves = (pl.ds(0, half), pl.ds(half, half))
    is_key = (row == 0).astype(F32)
    landed(recvkv, c_recv.at[0], sibling)
    kv_sum = (acckv_m[...] + recvkv[...]) * scale_col[...]
    cos_kv = cosine[...] * is_key + (1.0 - is_key)
    kv[row, 0] = (kv_sum * cos_kv + pltpu.roll(kv_sum, HD // 2, 1) * (sine[...] * is_key)).astype(BF16)

    def over(source, target, part, sem, step):
        piece = halves[part]
        launch(
            remote(kv.at[row, source, piece], kv.at[row, target, piece], x_send.at[sem], x_recv.at[sem], along(step))
        )

    def arrived(target, part, sem, step):
        landed(kv.at[row, target, halves[part]], x_recv.at[sem], along(-step))

    def across(target, sem):
        launch(remote(kv.at[row, target], kv.at[row, target], c_send.at[sem], c_recv.at[sem], sibling))

    over(0, 1, 0, 0, 1)
    over(0, 3, 1, 1, -1)
    over(0, 1, 1, 2, 1)
    over(0, 3, 0, 3, -1)
    across(0, 2)

    landed(recvq, c_recv.at[7], sibling)
    q_sum = (accq_m[...] + recvq[...]) * scale_col[...]
    qbuf[...] = (q_sum * cosine[...] + pltpu.roll(q_sum, HD // 2, 1) * sine[...]).astype(BF16)
    score_scale = 1.0 / math.sqrt(HD)

    def attend(k, part=None):
        size = SLAB if part is None else half
        keys = pl.ds(0, SLAB) if part is None else halves[part]
        from_seq = lax.rem(seq + 4 - k, 4)
        place = pl.ds(pl.multiple_of(from_seq * SLAB + (part or 0) * half, half), size)
        key_ids = ids[:, place].astype(F32)
        open_to = jnp.where(clean[:, place] == 1, 1e9, key_ids)
        scores = dot_nt(qbuf[...], kv[0, k, keys, :]) * score_scale
        mine = own_ids[:, :1]
        visible = (mine >= key_ids) & (mine <= open_to)
        weights = jnp.where(visible, jnp.exp(scores), 0.0)
        share = weights[:, :HD]
        for first in range(HD, size, HD):
            share = share + weights[:, first : first + HD]
        den[...] += share
        num[...] += dot(weights.astype(BF16), kv[1, k, keys, :])

    arrived(1, 0, 0, 1)
    over(1, 2, 0, 4, 1)
    arrived(3, 1, 1, -1)
    over(3, 2, 1, 5, -1)
    landed(kv.at[other, 0], c_recv.at[2], sibling)
    arrived(1, 1, 2, 1)
    across(1, 3)
    arrived(3, 0, 3, -1)
    across(3, 4)
    attend(0)
    landed(kv.at[other, 1], c_recv.at[3], sibling)
    attend(1)
    arrived(2, 0, 4, 1)
    arrived(2, 1, 5, -1)
    across(2, 5)
    landed(kv.at[other, 3], c_recv.at[4], sibling)
    attend(3)
    landed(kv.at[other, 2], c_recv.at[5], sibling)
    attend(2)

    att[0] = (num[...] / jnp.sum(den[...], axis=1, keepdims=True)).astype(BF16)
    launch(remote(att.at[0], att.at[1], c_send.at[6], c_recv.at[6], sibling))
    for copy in loads[9:]:
        copy.wait()
    landed(att.at[1], c_recv.at[6], sibling)

    for p, n in REDUCE:
        first, rows = ROWS[p]
        block = pl.ds(first, rows)
        left = jnp.concatenate([att[0, block, :], att[1, block, :]], axis=1)
        value = dot(left, wo[:, dyn(origin(n), CH)])
        for e in DOWN.get((p, n), []):
            _, _, below, step, part = EDGES[e]
            piece = pl.ds(part.start, part.stop - part.start)
            landed(rbuf.at[slot(below), piece, :], r_recv.at[e], plane(step))
            term = rbuf[slot(below), piece, :].astype(F32)
            if part == WHOLE[p]:
                value = value + term
            elif part.start == first:
                cut = part.stop - first
                value = jnp.concatenate([value[:cut] + term, value[cut:]], axis=0)
            else:
                cut = part.start - first
                value = jnp.concatenate([value[:cut], value[cut:] + term], axis=0)
        if n == (0, 0):
            out[block, :] = value.astype(BF16)
            continue
        sbuf[slot(n), block, :] = value.astype(BF16)
        for e in UP[(p, n)]:
            _, _, _, step, part = EDGES[e]
            piece = pl.ds(part.start, part.stop - part.start)
            launch(
                remote(
                    sbuf.at[slot(n), piece, :], rbuf.at[slot(n), piece, :],
                    r_send.at[e], r_recv.at[e], plane((-step[0], -step[1])),
                )
            )

    for copy in sent:
        copy.wait_send()


def shards(activations, norm_gain, query_weight, kv_weight, out_weight, block_ids, clean_mask):
    features = query_weight.shape[0]
    length = block_ids.shape[0]
    vmem = pl.BlockSpec(memory_space=pltpu.VMEM)
    hbm = pl.BlockSpec(memory_space=pl.ANY)
    dma = pltpu.SemaphoreType.DMA
    edges = len(EDGES)
    tokens_f32 = pltpu.VMEM((SLAB, HD), F32)
    within, starts = rope_tables()
    return pl.pallas_call(
        kernel,
        out_shape=jax.ShapeDtypeStruct((SLAB, CH), BF16),
        in_specs=[hbm] * 9,
        out_specs=vmem,
        scratch_shapes=[
            pltpu.VMEM((SLAB, CH), BF16),
            pltpu.VMEM((1, CH), F32),
            pltpu.VMEM((1, length), jnp.int32),
            pltpu.VMEM((1, length), jnp.int32),
            tokens_f32,
            pltpu.VMEM((8, HD), F32),
            pltpu.VMEM((SLAB, CH), BF16),
            pltpu.VMEM((NZ * NY, SLAB, CH), BF16),
            pltpu.VMEM((features, 2 * HD), BF16),
            pltpu.VMEM((features, 2, HD), BF16),
            pltpu.VMEM((features, 2 * HD), BF16),
            pltpu.VMEM((2 * HD, out_weight.shape[1]), BF16),
            pltpu.VMEM((2 * CH, 2 * CH), BF16),
            tokens_f32, tokens_f32, tokens_f32, tokens_f32,
            tokens_f32, tokens_f32, tokens_f32, tokens_f32,
            tokens_f32, tokens_f32,
            pltpu.VMEM((SLAB, HD), BF16),
            pltpu.VMEM((2, 4, SLAB, HD), BF16),
            tokens_f32, tokens_f32,
            pltpu.VMEM((2, SLAB, HD), BF16),
            pltpu.VMEM((NZ * NY, SLAB, CH), BF16),
            pltpu.VMEM((NZ * NY, SLAB, CH), BF16),
            pltpu.VMEM((NZ, 8, SLAB), F32),
            pltpu.VMEM((NY, 8, SLAB), F32),
            pltpu.VMEM((2, 8, SLAB), F32),
            dma((edges,)), dma((edges,)), dma((edges,)), dma((edges,)),
            dma((12,)), dma((12,)), dma((6,)), dma((6,)), dma((8,)), dma((8,)), dma((11,)),
        ],
        compiler_params=pltpu.CompilerParams(
            collective_id=0, has_side_effects=True, vmem_limit_bytes=VMEM_LIMIT
        ),
        name="layer",
    )(
        activations,
        norm_gain.reshape(1, CH),
        query_weight,
        kv_weight,
        out_weight,
        block_ids.reshape(1, length),
        clean_mask.reshape(1, length),
        jnp.asarray(within),
        jnp.asarray(starts),
    )


def solution(mesh):
    placed = (
        P("seq", ("row", "col")),
        P(("row", "col")),
        P("row", "col"),
        P("row", None, None),
        P("col", "row"),
        P(),
        P(),
    )
    return jax.shard_map(
        shards, mesh=mesh, in_specs=placed, out_specs=P("seq", ("row", "col")), check_vma=False
    )
```

time: 127 us -> 122 us (0.961)
  Pallas kernels: 125 us -> 120 us
    pallas_call x1, Pallas kernels: 125 us -> 120 us  [shards(): pl.pallas_call(kernel, out_shape=jax.ShapeDtypeStruct((SLAB, CH), BF16),...]
where the time goes in v2:
time: 122 us
  Pallas kernels  120 us (98%)
  local copies, waits for them, and re-layouts  1.67 us (1%)
    pallas_call x1, Pallas kernels, shards(): pl.pallas_call(kernel, out_shape=jax.ShapeDtypeStruct((SLAB, CH), BF16),...  120 us

profile of v2, /device:TPU:1, one launch (start us, length us, event | category | flops | bytes accessed | tf_op | source)
XLA Modules:
  0.0 121.6 jit_solution(5588898300802773640)
XLA Ops:
  0.0 119.9 %layer.1 = bf16[512,256]{1,0:T(8,128)(2,1)} custom-call(bf16[512,256]{1,0:T(8,128)(2,1)} %act_h.1, f32[1,256]{1,0:T(1,128)} %bitcast.5, bf16[8192,256]{1,0:T(8,128)(2,1)} %wq_h.1, bf16[8192,2,512]{2,1,0:T(2,128)(2,1)} %kv_h.1, bf16[256,8192]{1,0:T(8,128)(2,1)} %wo_h.1, s32[1,2048]{1,0:T(1,128)} %bitcast.3, s32[1,2048]{1,0:T(1,128)} %bitcast.4, ...), custom_call_target="tpu_custom_call" | custom-call | tf_op jit(solution)/shard_map/layer/pallas_call | solution.py:531
  119.9 1.7 %copy.11 = bf16[512,256]{1,0:T(8,128)(2,1)} copy(bf16[512,256]{1,0:T(8,128)(2,1)} %layer.1) | data formatting | bytes 524288

commit v3 on v2

--- a/solution.py
+++ b/solution.py
@@ -38,7 +38,7 @@
     return (n[0] % NZ) * NY + n[1] % NY
 
 
-HOP_US = 1.7
+HOP_US = 1.5
 COMP_US = 0.3
 LOADED_US = 8.0
 HALVED = True
@@ -101,7 +101,7 @@
 
 def link_us(e):
     rows = EDGES[e][4]
-    return (rows.stop - rows.start) * CH * 2 * 2 / 95e3
+    return (rows.stop - rows.start) * CH * 2 * 2 / 97e3
 
 
 def tail_down(key):
@@ -193,6 +193,7 @@
 
 GATHER, GATHER_US = plan_gather()
 REDUCE, REDUCE_US = plan_reduce()
+LAST_COMP = [max(i for i, event in enumerate(GATHER) if event[:2] == ("comp", part)) for part in (0, 1)]
 RECVS = [i for i, event in enumerate(GATHER) if event[0] == "recv"]
 FIRST_AT, SQUARES_AT = RECVS[4], (RECVS[-18], RECVS[-11], RECVS[-5])
 
@@ -329,7 +330,7 @@
 
     apart = set()
 
-    def compute(pair, n):
+    def compute(pair, n, last):
         if not apart:
             for copy in loads[2:5]:
                 copy.wait()
@@ -345,6 +346,8 @@
         theirs = dot(x, jnp.concatenate([wkv[at, pl.ds(HD, HD)], wq[at, pl.ds(HD, HD)]], axis=1))
         acckv_o[block, :] += theirs[:, :HD]
         accq_o[block, :] += theirs[:, HD:]
+        if last:
+            launch(remote(acckv_o.at[block, :], recvkv.at[block, :], c_send.at[8 * pair], c_recv.at[8 * pair], sibling))
         mine = dot(x, jnp.concatenate([wkv[at, pl.ds(0, HD)], wq[at, pl.ds(0, HD)]], axis=1))
         acckv_m[block, :] += mine[:, :HD]
         accq_m[block, :] += mine[:, HD:]
@@ -385,7 +388,7 @@
             scaling = lax.rsqrt(squares[:1] / D + norm_eps)
             scale_col[...] = jnp.broadcast_to(scaling, (HD, SLAB)).T
         if event[0] == "comp":
-            compute(event[1], event[2])
+            compute(event[1], event[2], position == LAST_COMP[event[1]])
             continue
         if event[0] == "send":
             send(event[1])
@@ -406,13 +409,14 @@
                 sqy[0] = total
                 sqy_forward(0)
 
-    launch(remote(acckv_o, recvkv, c_send.at[0], c_recv.at[0], sibling))
     launch(remote(accq_o, recvq, c_send.at[7], c_recv.at[7], sibling))
 
     half = SLAB // 2
     halves = (pl.ds(0, half), pl.ds(half, half))
     is_key = (row == 0).astype(F32)
-    landed(recvkv, c_recv.at[0], sibling)
+    for part in (1, 0):
+        block = pl.ds(*ROWS[part])
+        landed(recvkv.at[block, :], c_recv.at[8 * part], sibling)
     kv_sum = (acckv_m[...] + recvkv[...]) * scale_col[...]
     cos_kv = cosine[...] * is_key + (1.0 - is_key)
     kv[row, 0] = (kv_sum * cos_kv + pltpu.roll(kv_sum, HD // 2, 1) * (sine[...] * is_key)).astype(BF16)
@@ -469,13 +473,15 @@
     attend(0)
     landed(kv.at[other, 1], c_recv.at[3], sibling)
     attend(1)
-    arrived(2, 0, 4, 1)
-    arrived(2, 1, 5, -1)
-    across(2, 5)
+    for part, step in ((0, 1), (1, -1)):
+        arrived(2, part, 4 + part, step)
+        piece = kv.at[row, 2, halves[part]]
+        launch(remote(piece, piece, c_send.at[5 + 4 * part], c_recv.at[5 + 4 * part], sibling))
     landed(kv.at[other, 3], c_recv.at[4], sibling)
     attend(3)
-    landed(kv.at[other, 2], c_recv.at[5], sibling)
-    attend(2)
+    for part in (0, 1):
+        landed(kv.at[other, 2, halves[part]], c_recv.at[5 + 4 * part], sibling)
+        attend(2, part)
 
     att[0] = (num[...] / jnp.sum(den[...], axis=1, keepdims=True)).astype(BF16)
     launch(remote(att.at[0], att.at[1], c_send.at[6], c_recv.at[6], sibling))
@@ -560,7 +566,7 @@
             pltpu.VMEM((NY, 8, SLAB), F32),
             pltpu.VMEM((2, 8, SLAB), F32),
             dma((edges,)), dma((edges,)), dma((edges,)), dma((edges,)),
-            dma((12,)), dma((12,)), dma((6,)), dma((6,)), dma((8,)), dma((8,)), dma((11,)),
+            dma((12,)), dma((12,)), dma((6,)), dma((6,)), dma((10,)), dma((10,)), dma((11,)),
         ],
         compiler_params=pltpu.CompilerParams(
             collective_id=0, has_side_effects=True, vmem_limit_bytes=VMEM_LIMIT

time: 122 us -> 122 us (level)
  no operation moved by 1% of the time
where the time goes in v3:
time: 122 us
  Pallas kernels  120 us (98%)
  local copies, waits for them, and re-layouts  1.67 us (1%)
    pallas_call x1, Pallas kernels, shards(): pl.pallas_call(kernel, out_shape=jax.ShapeDtypeStruct((SLAB, CH), BF16),...  120 us

profile of v3, /device:TPU:1, one launch (start us, length us, event | category | flops | bytes accessed | tf_op | source)
XLA Modules:
  0.0 121.9 jit_solution(153901918977502002)
XLA Ops:
  0.0 120.2 %layer.1 = bf16[512,256]{1,0:T(8,128)(2,1)} custom-call(bf16[512,256]{1,0:T(8,128)(2,1)} %act_h.1, f32[1,256]{1,0:T(1,128)} %bitcast.5, bf16[8192,256]{1,0:T(8,128)(2,1)} %wq_h.1, bf16[8192,2,512]{2,1,0:T(2,128)(2,1)} %kv_h.1, bf16[256,8192]{1,0:T(8,128)(2,1)} %wo_h.1, s32[1,2048]{1,0:T(1,128)} %bitcast.3, s32[1,2048]{1,0:T(1,128)} %bitcast.4, ...), custom_call_target="tpu_custom_call" | custom-call | tf_op jit(solution)/shard_map/layer/pallas_call | solution.py:537
  120.2 1.7 %copy.11 = bf16[512,256]{1,0:T(8,128)(2,1)} copy(bf16[512,256]{1,0:T(8,128)(2,1)} %layer.1) | data formatting | bytes 524288

commit v4 on v3

--- a/solution.py
+++ b/solution.py
@@ -483,15 +483,22 @@
         landed(kv.at[other, 2, halves[part]], c_recv.at[5 + 4 * part], sibling)
         attend(2, part)
 
-    att[0] = (num[...] / jnp.sum(den[...], axis=1, keepdims=True)).astype(BF16)
-    launch(remote(att.at[0], att.at[1], c_send.at[6], c_recv.at[6], sibling))
+    lead = REDUCE[0][0]
+    for part in (lead, 1 - lead):
+        block = pl.ds(*ROWS[part])
+        att[0, block, :] = (num[block, :] / jnp.sum(den[block, :], axis=1, keepdims=True)).astype(BF16)
+        k = 6 + 4 * part
+        launch(remote(att.at[0, block, :], att.at[1, block, :], c_send.at[k], c_recv.at[k], sibling))
     for copy in loads[9:]:
         copy.wait()
-    landed(att.at[1], c_recv.at[6], sibling)
+    attended = set()
 
     for p, n in REDUCE:
         first, rows = ROWS[p]
         block = pl.ds(first, rows)
+        if p not in attended:
+            attended.add(p)
+            landed(att.at[1, block, :], c_recv.at[6 + 4 * p], sibling)
         left = jnp.concatenate([att[0, block, :], att[1, block, :]], axis=1)
         value = dot(left, wo[:, dyn(origin(n), CH)])
         for e in DOWN.get((p, n), []):
@@ -566,7 +573,7 @@
             pltpu.VMEM((NY, 8, SLAB), F32),
             pltpu.VMEM((2, 8, SLAB), F32),
             dma((edges,)), dma((edges,)), dma((edges,)), dma((edges,)),
-            dma((12,)), dma((12,)), dma((6,)), dma((6,)), dma((10,)), dma((10,)), dma((11,)),
+            dma((12,)), dma((12,)), dma((6,)), dma((6,)), dma((11,)), dma((11,)), dma((11,)),
         ],
         compiler_params=pltpu.CompilerParams(
             collective_id=0, has_side_effects=True, vmem_limit_bytes=VMEM_LIMIT

time: 122 us -> 122 us (level)
  no operation moved by 1% of the time
where the time goes in v4:
time: 122 us
  Pallas kernels  120 us (98%)
  local copies, waits for them, and re-layouts  1.67 us (1%)
    pallas_call x1, Pallas kernels, shards(): pl.pallas_call(kernel, out_shape=jax.ShapeDtypeStruct((SLAB, CH), BF16),...  120 us

profile of v4, /device:TPU:1, one launch (start us, length us, event | category | flops | bytes accessed | tf_op | source)
XLA Modules:
  0.0 121.9 jit_solution(16826408442385695753)
XLA Ops:
  0.0 120.2 %layer.1 = bf16[512,256]{1,0:T(8,128)(2,1)} custom-call(bf16[512,256]{1,0:T(8,128)(2,1)} %act_h.1, f32[1,256]{1,0:T(1,128)} %bitcast.5, bf16[8192,256]{1,0:T(8,128)(2,1)} %wq_h.1, bf16[8192,2,512]{2,1,0:T(2,128)(2,1)} %kv_h.1, bf16[256,8192]{1,0:T(8,128)(2,1)} %wo_h.1, s32[1,2048]{1,0:T(1,128)} %bitcast.3, s32[1,2048]{1,0:T(1,128)} %bitcast.4, ...), custom_call_target="tpu_custom_call" | custom-call | tf_op jit(solution)/shard_map/layer/pallas_call | solution.py:544
  120.2 1.7 %copy.11 = bf16[512,256]{1,0:T(8,128)(2,1)} copy(bf16[512,256]{1,0:T(8,128)(2,1)} %layer.1) | data formatting | bytes 524288
